TPU v7x, 32 devices: a whole 2x2x4 slice. The times are simulated.
32 devices in a mesh: groups: 2 (over y), cand: 4 (over z), tensor: 4 (over x, core).
Axes of the slice: x: 2, y: 2, z: 4, core: 2. Of those that a mesh axis runs over, the one named last changes fastest.
Arguments:
- response_latest_embeddings: bfloat16 [16, 384, 8192], P(('groups', 'cand'), None, 'tensor'), parts along dimension 0, may hold values from -6 to 6
- critic_probe_projector: bfloat16 [8192, 4096], P('cand', 'tensor'), may hold values from -0.0625 to 0.0625
- critic_pair_projector: bfloat16 [8192, 2048], P('cand', 'tensor'), may hold values from -0.0625 to 0.0625
- critic_stored_pairs: bfloat16 [16, 2048, 2048], P(('groups', 'cand'), None, 'tensor'), parts along dimension 0, may hold values from -1000 to 1000
- critic_grading_vector: float32 [4096], P('tensor'), may hold values from -6 to 6
- actor_stored_pairs: bfloat16 [16, 2048, 8, 256], P(('groups', 'cand'), None, 'tensor'), parts along dimension 0, may hold values from -1000 to 1000
- filled_extents: int32 [16], P('groups'), parts along dimension 0, may hold values from 1 to 2048, as said below
- kept_responses: int32 [8], P('groups'), parts along dimension 0, may hold values from 0 to 7, as said below
- actor_latest_probes: bfloat16 [8, 4, 4096], P(('groups', 'cand'), None, 'tensor'), parts along dimension 0, may hold values from -6 to 6
- actor_latest_pairs: bfloat16 [8, 4, 2048], P(('groups', 'cand'), None, 'tensor'), parts along dimension 0, may hold values from -6 to 6
Outputs:
- token_rewards: float32 [16, 384], P(('groups', 'cand')), parts along dimension 0
- actor_mixing_result: bfloat16 [8, 4, 4096], P(('groups', 'cand'), None, 'tensor'), parts along dimension 0
There are 2 independent parts, one for each index of `groups`. A program takes and returns all parts, laid end to end along the dimension named above; an argument that names none is the same for every part. Nothing has to cross between parts.
Inputs may be any that keep to these rules, and one draw needn't show every extreme that they name: `kept_responses`: distinct candidate ids, always including 0 and 7. `filled_extents`: some candidate has exactly 2048 live tokens.
All inputs are finite; a program needn't handle non-finite values.
Results may differ from a plain program's by a relative error of at most 0.012.
The roundings to bfloat16 on the way count: a program that leaves them out, or rounds other values in their place, can miss the bound.
Values may be sent and summed in bfloat16 or wider, within the bound.
A program may use at most 128 MiB of HBM per device.

v0:
```python
import jax
import jax.numpy as jnp
from jax import lax
from jax.sharding import PartitionSpec as P

HD = 128
masked_value = -1e30


def local(
    response_latest_embeddings,
    critic_probe_projector,
    critic_pair_projector,
    critic_stored_pairs,
    critic_grading_vector,
    actor_stored_pairs,
    filled_extents,
    kept_responses,
    actor_latest_probes,
    actor_latest_pairs,
):
    cand_here = response_latest_embeddings.shape[0]
    span_len = response_latest_embeddings.shape[1]
    key_scale = HD ** (-0.5)
    whole_states = lax.all_gather(response_latest_embeddings, "tensor", axis=2, tiled=True)
    full_width = whole_states.shape[2]
    tok_rows = whole_states.reshape(cand_here * span_len, full_width)
    query_cols = critic_probe_projector.shape[1]
    keyval_cols = critic_pair_projector.shape[1]
    query_sum = jnp.dot(
        tok_rows,
        lax.all_gather(critic_probe_projector, "cand", axis=0, tiled=True),
        preferred_element_type=jnp.float32,
    )
    keyval_sum = jnp.dot(
        tok_rows,
        lax.all_gather(critic_pair_projector, "cand", axis=0, tiled=True),
        preferred_element_type=jnp.float32,
    )
    heads_here = query_cols // HD
    groups_here = keyval_cols // (2 * HD)
    per_group = heads_here // groups_here
    query_heads = query_sum.astype(jnp.bfloat16).reshape(
        cand_here, span_len, groups_here, per_group, HD
    )
    keyval = keyval_sum.astype(jnp.bfloat16).reshape(cand_here, span_len, groups_here, 2 * HD)
    context = critic_stored_pairs.shape[1]
    cached = critic_stored_pairs.reshape(cand_here, context, groups_here, 2 * HD)
    every_key = jnp.concatenate([cached, keyval], axis=1)
    causal = lax.broadcasted_iota(jnp.int32, (span_len, span_len), 0) >= lax.broadcasted_iota(
        jnp.int32, (span_len, span_len), 1
    )
    visible = jnp.concatenate([jnp.ones((span_len, context), dtype=bool), causal], axis=1)

    def score_one(entry_pair):
        queries, keys_values = entry_pair
        scores = (
            jnp.einsum(
                "tkgd,skd->kgts", queries, keys_values[..., :HD], preferred_element_type=jnp.float32
            )
            * key_scale
        )
        scores = jnp.where(visible, scores, masked_value)
        rounded = jax.nn.softmax(scores, axis=-1).astype(jnp.bfloat16)
        heads_out = jnp.einsum(
            "kgts,skd->tkgd", rounded, keys_values[..., HD:], preferred_element_type=jnp.float32
        )
        return jnp.dot(
            heads_out.reshape(span_len, heads_here * HD),
            critic_grading_vector,
            precision=lax.Precision.HIGHEST,
        )

    partial_reward = lax.map(score_one, (query_heads, every_key))
    token_rewards = lax.psum(partial_reward, "tensor")
    device_here = lax.axis_index("cand")
    lane_number = kept_responses.shape[0]
    new_count = actor_latest_probes.shape[1]
    kv_here = actor_stored_pairs.shape[2]
    policy_heads = actor_latest_probes.shape[2] // HD
    policy_group = policy_heads // kv_here
    cache_len = actor_stored_pairs.shape[1]
    causal_new = lax.broadcasted_iota(jnp.int32, (new_count, new_count), 0) >= lax.broadcasted_iota(
        jnp.int32, (new_count, new_count), 1
    )
    all_queries, all_fresh = (
        lax.all_gather(actor_latest_probes, "cand", axis=0, tiled=True),
        lax.all_gather(actor_latest_pairs, "cand", axis=0, tiled=True),
    )
    ids_here = device_here * cand_here + lax.broadcasted_iota(jnp.int32, (cand_here,), 0)
    matched = kept_responses[None, :] == ids_here[:, None]
    slot_index = jnp.sum(
        jnp.where(matched, lax.broadcasted_iota(jnp.int32, (cand_here, lane_number), 1), 0), axis=1
    )
    own_queries = jnp.take(all_queries, slot_index, axis=0).reshape(
        cand_here, new_count, kv_here, policy_group, HD
    )
    own_fresh = jnp.take(all_fresh, slot_index, axis=0).reshape(
        cand_here, new_count, kv_here, 2 * HD
    )
    sequence_places = lax.broadcasted_iota(jnp.int32, (cache_len,), 0)
    living_response_flags = sequence_places[None, :] < jnp.take(filled_extents, ids_here)[:, None]
    living_response_flags = living_response_flags[:, None, None, None, :]
    scores = (
        jnp.einsum(
            "cikgd,ctkd->ckgit",
            own_queries,
            actor_stored_pairs[..., :HD],
            preferred_element_type=jnp.float32,
        )
        * key_scale
    )
    scores = jnp.where(living_response_flags, scores, masked_value)
    fresh_scores = (
        jnp.einsum(
            "cikgd,cjkd->ckgij",
            own_queries,
            own_fresh[..., :HD],
            preferred_element_type=jnp.float32,
        )
        * key_scale
    )
    fresh_scores = jnp.where(causal_new, fresh_scores, masked_value)
    peak_score = jnp.maximum(jnp.max(scores, axis=-1), jnp.max(fresh_scores, axis=-1))
    old_weights = jnp.where(living_response_flags, jnp.exp(scores - peak_score[..., None]), 0.0)
    fresh_weights = jnp.where(causal_new, jnp.exp(fresh_scores - peak_score[..., None]), 0.0)
    denominator = jnp.sum(old_weights, axis=-1) + jnp.sum(fresh_weights, axis=-1)
    numerator = jnp.einsum(
        "ckgit,ctkd->ckgid",
        old_weights,
        actor_stored_pairs[..., HD:],
        preferred_element_type=jnp.float32,
    )
    numerator = numerator + jnp.einsum(
        "ckgij,cjkd->ckgid", fresh_weights, own_fresh[..., HD:], preferred_element_type=jnp.float32
    )
    result = numerator / denominator[..., None]
    flattened = jnp.transpose(result, (0, 3, 1, 2, 4)).reshape(
        cand_here, new_count * policy_heads * HD
    )
    placed = jnp.einsum(
        "cs,cx->sx", matched.astype(jnp.float32), flattened, precision=lax.Precision.HIGHEST
    )
    slot_rows = lax.psum_scatter(
        placed.reshape(lane_number, new_count, policy_heads * HD).astype(jnp.bfloat16),
        "cand",
        scatter_dimension=0,
        tiled=True,
    )
    return (token_rewards, slot_rows)


def solution(mesh):
    placed = (
        P(("groups", "cand"), None, "tensor"),
        P("cand", "tensor"),
        P("cand", "tensor"),
        P(("groups", "cand"), None, "tensor"),
        P("tensor"),
        P(("groups", "cand"), None, "tensor", None),
        P("groups"),
        P("groups"),
        P(("groups", "cand"), None, "tensor"),
        P(("groups", "cand"), None, "tensor"),
    )
    return jax.shard_map(
        local,
        mesh=mesh,
        in_specs=placed,
        out_specs=(P(("groups", "cand"), None), P(("groups", "cand"), None, "tensor")),
        check_vma=False,
    )
```

profile of v0, /device:TPU:0, one launch (start us, length us, event | category | flops | bytes accessed | tf_op | source)
XLA Modules:
  0.0 638.4 jit_solution(14081413601439974650)
XLA Ops:
  7.2 0.0 copy-start
  7.2 0.0 all-gather.6.cloned.1.call-start
  7.2 0.7 all-gather.6.cloned.1.call-update
  7.9 0.0 all-gather.4.cloned.1.call-start
  8.0 0.7 all-gather.4.cloned.1.call-update
  8.7 0.0 all-gather.8.cloned.1.call-start
  8.7 0.7 all-gather.8.cloned.1.call-update
  9.4 0.0 copy-start.4
  9.4 0.0 copy-start.6
  9.4 0.0 copy-start.5
  9.5 6.3 copy.40
  15.8 0.0 copy-done
  15.8 0.6 gather_fusion
  16.4 0.0 copy-done.4
  16.4 15.2 %all_gather.18 = bf16[4,4,1024]{2,1,0:T(4,128)(2,1)S(1)} all-gather(bf16[1,4,1024]{2,1,0:T(4,128)(2,1)S(1)} %copy-done.4), channel_id=1, replica_groups=mesh['groups'=2,'cand'=4,'tensor'=4] {'cand'}, dimensions={0}, use_global_device_ids=true | all-gather | bytes 40960 | tf_op jit(solution)/shard_map/all_gather | solution.py:87
  31.7 0.0 copy-done.6
  31.7 0.2 fusion.26
  31.9 0.6 gather_fusion.1
  32.5 19.5 %all_gather.19 = bf16[4,4,512]{2,1,0:T(4,128)(2,1)S(1)} all-gather(bf16[1,4,512]{2,1,0:T(4,128)(2,1)S(1)} %copy-done.5), channel_id=1, replica_groups=mesh['groups'=2,'cand'=4,'tensor'=4] {'cand'}, dimensions={0}, use_global_device_ids=true | all-gather | bytes 20480 | tf_op jit(solution)/shard_map/all_gather | solution.py:88
  51.9 0.6 gather_fusion.2
  52.5 0.1 broadcast_select_fusion
  52.6 0.3 fusion.36
  53.0 0.1 iota_compare_fusion.1
  53.0 4.7 fusion.34
  57.8 0.0 copy-start.7
  57.8 0.8 fusion.35
  58.6 0.1 fusion.22
  58.7 0.4 fusion.18
  59.1 0.6 fusion.13
  59.7 0.3 fusion.15
  60.0 0.3 convolution_convert_fusion.2
  60.4 1.2 concatenate.7
  61.6 0.0 copy-done.7
  61.6 0.6 dynamic-slice
  62.2 24.7 %all-reduce.1 = bf16[4,4,1024]{2,1,0:T(4,128)(2,1)S(1)} all-reduce(bf16[4,4,1024]{2,1,0:T(4,128)(2,1)S(1)} %copy.52), channel_id=2, replica_groups=mesh['groups'=2,'cand'=4,'tensor'=4] {'cand'}, use_global_device_ids=true, to_apply=%region_10.11.clone | all-reduce | flops 16384 | bytes 65536
  86.9 1.2 constant_dynamic-slice_fusion.2
  88.1 75.4 %all-gather.6.cloned.1.call-done = bf16[8192,512]{1,0:T(8,128)(2,1)} async-done(((bf16[2048,512]{1,0:T(8,128)(2,1)}), bf16[8192,512]{1,0:T(8,128)(2,1)}) %all-gather.6.cloned.1.call-update) | async-done | bytes 8388624 | tf_op jit(solution)/shard_map/all_gather | solution.py:37
  163.5 81.9 %all-gather.4.cloned.1.call-done = bf16[2,384,8192]{2,1,0:T(8,128)(2,1)} async-done(((bf16[2,384,2048]{2,1,0:T(8,128)(2,1)}), bf16[2,384,8192]{2,1,0:T(8,128)(2,1)}) %all-gather.4.cloned.1.call-update) | async-done | bytes 12582928 | tf_op jit(solution)/shard_map/all_gather | solution.py:25
  245.4 12.0 %convolution_convert_fusion.1 = bf16[768,512]{1,0:T(8,128)(2,1)S(1)} fusion(bf16[768,8192]{1,0:T(8,128)(2,1)} %bitcast.129, bf16[8192,512]{1,0:T(8,128)(2,1)} %all-gather.6.cloned.1.call-done), kind=kOutput, calls=%fused_computation.29 | convolution fusion | flops 6442844160 | bytes 21757952 | tf_op jit(solution)/shard_map/dot_general | solution.py:35
  257.4 0.2 reshape.109
  257.6 0.6 copy.41
  258.2 5.4 pad_maximum_fusion
  263.7 270.1 %all-gather.8.cloned.1.call-done = bf16[8192,1024]{1,0:T(8,128)(2,1)} async-done(((bf16[2048,1024]{1,0:T(8,128)(2,1)}), bf16[8192,1024]{1,0:T(8,128)(2,1)}) %all-gather.8.cloned.1.call-update) | async-done | bytes 16777232 | tf_op jit(solution)/shard_map/all_gather | solution.py:32
  533.7 18.7 %convolution_convert_fusion = bf16[768,1024]{1,0:T(8,128)(2,1)S(1)} fusion(bf16[768,8192]{1,0:T(8,128)(2,1)} %bitcast.130, bf16[8192,1024]{1,0:T(8,128)(2,1)} %all-gather.8.cloned.1.call-done), kind=kOutput, calls=%fused_computation.28 | convolution fusion | flops 12885688320 | bytes 30932992 | tf_op jit(solution)/shard_map/dot_general | solution.py:30
  552.5 2.4 reshape.110
  554.9 69.6 %while.10 = (s32[]{:T(128)}, f32[2,384]{1,0:T(2,128)S(1)}, bf16[2,2432,2,256]{1,3,2,0:T(8,128)(2,1)}, pred[384,2432]{0,1:T(8,128)(4,1)}, bf16[2,384,2,4,128]{4,3...) while((s32[]{:T(128)}, f32[2,384]{1,0:T(2,128)S(1)}, bf16[2,2432,2,256]{1,3,2,0:T(8,128)(2,1)}, ...), condition=%wide.region_3.4_spmd, body=%wide.region_0.3_spmd.sunk | while | flops 3874753024 | bytes 88654472 | solution.py:74
  554.9 1.9 constant_dynamic-slice_fusion.5
  556.7 2.6 copy.94
  559.4 1.4 constant_dynamic-slice_fusion.6
  560.8 0.0 copy-start.2
  560.8 17.0 %fusion.52 = (f32[2,4,384]{2,1,0:T(4,128)S(1)}, f32[2,4,384,2432]{2,3,1,0:T(8,128)}) fusion(pred[384,2432]{0,1:T(8,128)(4,1)} %get-tuple-element.139, bf16[2432,2,256]{2,0,1:T(8,128)(2,1)} %bitcast.122, bf16[1,384,2,4,128]{4,3,2,1,0:T(4,128)(2,1)S(1)} %constant_dynamic-slice_fusion.6), kind=kOutput, calls=%fused_computation.74.clone.1 | convolution fusion | flops 1942489472 | bytes 32862208 | tf_op jit(solution)/shard_map/while/body/eval_jaxpr/sub | solution.py:64
  577.8 10.9 %fusion.53 = f32[2,128,4,384]{3,1,2,0:T(8,128)S(1)} fusion(f32[2,4,384,2432]{2,3,1,0:T(8,128)} %get-tuple-element.118, f32[2,4,384]{2,1,0:T(4,128)S(1)} %get-tuple-element.119, bf16[2432,2,256]{2,0,1:T(8,128)(2,1)S(1)} %bitcast.123), kind=kOutput, calls=%fused_computation.11.clone.1 | convolution fusion | flops 1927544832 | bytes 32714752 | tf_op jit(solution)/shard_map/while/body/eval_jaxpr/kgts,skd->tkgd/dot_general | solution.py:65
  588.7 0.9 fusion.54
  589.6 0.1 dynamic_update_slice.5
  589.7 1.9 constant_dynamic-slice_fusion.5
  591.6 2.6 copy.94
  594.2 1.4 constant_dynamic-slice_fusion.6
  595.6 0.0 copy-start.2
  595.6 17.0 %fusion.52 = (f32[2,4,384]{2,1,0:T(4,128)S(1)}, f32[2,4,384,2432]{2,3,1,0:T(8,128)}) fusion(pred[384,2432]{0,1:T(8,128)(4,1)} %get-tuple-element.139, bf16[2432,2,256]{2,0,1:T(8,128)(2,1)} %bitcast.122, bf16[1,384,2,4,128]{4,3,2,1,0:T(4,128)(2,1)S(1)} %constant_dynamic-slice_fusion.6), kind=kOutput, calls=%fused_computation.74.clone.1 | convolution fusion | flops 1942489472 | bytes 32862208 | tf_op jit(solution)/shard_map/while/body/eval_jaxpr/sub | solution.py:64
  612.6 10.9 %fusion.53 = f32[2,128,4,384]{3,1,2,0:T(8,128)S(1)} fusion(f32[2,4,384,2432]{2,3,1,0:T(8,128)} %get-tuple-element.118, f32[2,4,384]{2,1,0:T(4,128)S(1)} %get-tuple-element.119, bf16[2432,2,256]{2,0,1:T(8,128)(2,1)S(1)} %bitcast.123), kind=kOutput, calls=%fused_computation.11.clone.1 | convolution fusion | flops 1927544832 | bytes 32714752 | tf_op jit(solution)/shard_map/while/body/eval_jaxpr/kgts,skd->tkgd/dot_general | solution.py:65
  623.5 0.9 fusion.54
  624.4 0.1 dynamic_update_slice.5
  624.5 0.0 copy-start.1
  624.5 7.4 %psum.7 = f32[2,384]{1,0:T(2,128)} all-reduce(f32[2,384]{1,0:T(2,128)S(1)} %get-tuple-element.34), channel_id=1, replica_groups=mesh['groups'=2,'cand'=4,'tensor'=4] {'tensor'}, use_global_device_ids=true, to_apply=%region_4.5 | all-reduce | flops 768 | bytes 6144 | tf_op jit(solution)/shard_map/psum | solution.py:75
  (21 shorter events, 0.2 us)
Async XLA Ops:
  7.2 8.6 %copy-start = (s32[8]{0:T(128)S(1)}, s32[8]{0:T(128)}, u32[]{:S(2)}) copy-start(s32[8]{0:T(128)} %param.18) | copy-start | bytes 100
  7.2 156.3 %all-gather.6.cloned.1.call-start = ((), (), s32[]{:S(2)}) async-start(), calls=%async_computation.1 | async-start | bytes 10485760 | tf_op jit(solution)/shard_map/all_gather | solution.py:37
  7.9 237.4 %all-gather.4.cloned.1.call-start = ((), (), s32[]{:S(2)}) async-start(), calls=%async_computation | async-start | bytes 15728640 | tf_op jit(solution)/shard_map/all_gather | solution.py:25
  8.7 525.1 %all-gather.8.cloned.1.call-start = ((), (), s32[]{:S(2)}) async-start(), calls=%async_computation.2 | async-start | bytes 20971520 | tf_op jit(solution)/shard_map/all_gather | solution.py:32
  9.4 7.0 %copy-start.4 = (bf16[1,4,1024]{2,1,0:T(4,128)(2,1)S(1)}, bf16[1,4,1024]{2,1,0:T(4,128)(2,1)}, u32[]{:S(2)}) copy-start(bf16[1,4,1024]{2,1,0:T(4,128)(2,1)} %param.20) | copy-start | bytes 24580
  9.4 22.2 %copy-start.6 = (s32[4]{0:T(128)S(1)}, s32[4]{0:T(128)}, u32[]{:S(2)}) copy-start(s32[4]{0:T(128)} %param.19) | copy-start | bytes 52
  9.4 23.0 %copy-start.5 = (bf16[1,4,512]{2,1,0:T(4,128)(2,1)S(1)}, bf16[1,4,512]{2,1,0:T(4,128)(2,1)}, u32[]{:S(2)}) copy-start(bf16[1,4,512]{2,1,0:T(4,128)(2,1)} %param.21) | copy-start | bytes 12292
  57.8 3.8 copy-start.7
  263.7 291.2 %copy-start.3 = (f32[1024]{0:T(1024)S(1)}, f32[1024]{0:T(1024)}, u32[]{:S(2)}) copy-start(f32[1024]{0:T(1024)} %param.16) | copy-start | bytes 12292
  560.8 17.0 %copy-start.2 = (bf16[1,2432,2,256]{3,1,2,0:T(8,128)(2,1)S(1)}, bf16[1,2432,2,256]{3,1,2,0:T(8,128)(2,1)}, u32[]{:S(2)}) copy-start(bf16[1,2432,2,256]{3,1,2,0:T(8,128)(2,1)} %copy.94) | copy-start | bytes 7471108 | tf_op jit(solution)/shard_map/while
  595.6 17.0 %copy-start.2 = (bf16[1,2432,2,256]{3,1,2,0:T(8,128)(2,1)S(1)}, bf16[1,2432,2,256]{3,1,2,0:T(8,128)(2,1)}, u32[]{:S(2)}) copy-start(bf16[1,2432,2,256]{3,1,2,0:T(8,128)(2,1)} %copy.94) | copy-start | bytes 7471108 | tf_op jit(solution)/shard_map/while
  624.5 7.4 %copy-start.1 = (s32[8]{0:T(128)S(1)}, s32[8]{0:T(128)}, u32[]{:S(2)}) copy-start(s32[8]{0:T(128)} %param.18) | copy-start | bytes 100
Sparse Core Ops, SparseCore 0:
  9.6 153.8 all-gather.5
  165.0 80.3 all-gather.3
  246.9 286.7 all-gather.7
where the time goes:
time: 639 us; the launch traced here: 638 us
  waiting for transfers between devices  429 us (67%)
  matrix products  90.7 us (14%)
  blocking collectives  66.8 us (10%)
  local copies, waits for them, and re-layouts  31 us (5%)
  between operations  14 us (2%)
    all_gather x1, waiting for transfers between devices, local(): lax.all_gather(critic_probe_projector, 'cand', axis=0, tiled=True)  270 us
    all_gather x1, waiting for transfers between devices, local(): lax.all_gather(response_latest_embeddings, 'tensor', axis=2, tiled=True)  81.9 us
    all_gather x1, waiting for transfers between devices, local(): lax.all_gather(critic_pair_projector, 'cand', axis=0, tiled=True)  75.4 us
    sub x2, matrix products, score_one(): rounded = jax.nn.softmax(scores, axis=-1).astype(jnp.bfloat16)  34 us
    unnamed x1, blocking collectives  24.7 us
    dot_general x2, matrix products, score_one(): jnp.einsum('kgts,skd->tkgd', rounded, keys_values[..., HD:], preferred_el...  21.8 us
    all_gather x1, blocking collectives, local(): lax.all_gather(actor_latest_pairs, 'cand', axis=0, tiled=True)  19.5 us
    dot_general x1, matrix products, local(): jnp.dot(tok_rows, lax.all_gather(critic_probe_projector, 'cand', axis=0,...  18.7 us
  transfers between devices with their start and end apart: 3, of which 3 were waited for; matrix products, arithmetic and copies ran while one was open for 6% of the time, Pallas kernels for 0%

commit v1 on v0

--- a/solution.py
+++ b/solution.py
@@ -22,7 +22,14 @@
     cand_here = response_latest_embeddings.shape[0]
     span_len = response_latest_embeddings.shape[1]
     key_scale = HD ** (-0.5)
-    whole_states = lax.all_gather(response_latest_embeddings, "tensor", axis=2, tiled=True)
+    ring = [response_latest_embeddings]
+    for hop in range(3):
+        ring.append(lax.ppermute(ring[-1], "tensor", [(dev, (dev + 1) % 4) for dev in range(4)]))
+    whole_states = jnp.roll(
+        jnp.concatenate(ring[::-1], axis=2),
+        (lax.axis_index("tensor") + 1) * ring[0].shape[2],
+        axis=2,
+    )
     full_width = whole_states.shape[2]
     tok_rows = whole_states.reshape(cand_here * span_len, full_width)
     query_cols = critic_probe_projector.shape[1]

time: 639 us -> 556 us (0.87)
  waiting for transfers between devices: 429 us -> 327 us
  local copies, waits for them, and re-layouts: 31 us -> 46.9 us
    all_gather x1 -> x0, waiting for transfers between devices: 81.9 us -> none  [local(): lax.all_gather(response_latest_embeddings, 'tensor', axis=2, tiled=True)]
    all_gather x1, waiting for transfers between devices: 75.4 us -> 2.92 us  [local(): lax.all_gather(critic_pair_projector, 'cand', axis=0, tiled=True)]
    ppermute x0 -> x3, waiting for transfers between devices: none -> 54.6 us  [local(): lax.ppermute(ring[-1], 'tensor', [(dev, (dev + 1) % 4) for dev in range(4)])]
    unnamed x17 -> x24, local copies, waits for them, and re-layouts: 8.13 us -> 18.4 us
  transfers between devices with their start and end apart: 3 -> 5, of which waited for: 3 -> 4; matrix products, arithmetic and copies ran while one was open for 6% -> 10% of each run, Pallas kernels for 0% -> 0%
where the time goes in v1:
time: 556 us; the launch traced here: 555 us
  waiting for transfers between devices  327 us (59%)
  matrix products  90.7 us (16%)
  blocking collectives  68.3 us (12%)
  local copies, waits for them, and re-layouts  46.9 us (8%)
  between operations  14.3 us (3%)
  other arithmetic  6.86 us (1%)
    all_gather x1, waiting for transfers between devices, local(): lax.all_gather(critic_probe_projector, 'cand', axis=0, tiled=True)  269 us
    ppermute x3, waiting for transfers between devices, local(): lax.ppermute(ring[-1], 'tensor', [(dev, (dev + 1) % 4) for dev in range(4)])  54.6 us
    sub x2, matrix products, score_one(): rounded = jax.nn.softmax(scores, axis=-1).astype(jnp.bfloat16)  34 us
    unnamed x1, blocking collectives  25.4 us
    dot_general x2, matrix products, score_one(): jnp.einsum('kgts,skd->tkgd', rounded, keys_values[..., HD:], preferred_el...  21.8 us
    dot_general x1, matrix products, local(): jnp.dot(tok_rows, lax.all_gather(critic_probe_projector, 'cand', axis=0,...  18.7 us
    all_gather x1, blocking collectives, local(): lax.all_gather(actor_latest_probes, 'cand', axis=0, tiled=True)  18.4 us
    unnamed x24, local copies, waits for them, and re-layouts  18.4 us
  transfers between devices with their start and end apart: 5, of which 4 were waited for; matrix products, arithmetic and copies ran while one was open for 10% of the time, Pallas kernels for 0%

profile of v1, /device:TPU:0, one launch (start us, length us, event | category | flops | bytes accessed | tf_op | source)
XLA Modules:
  0.0 555.3 jit_solution(18220946005844384471)
XLA Ops:
  7.2 0.0 copy-start
  7.2 0.0 all-gather.3.cloned.1.call-start
  7.2 0.7 all-gather.3.cloned.1.call-update
  7.9 0.0 all-gather.5.cloned.1.call-start
  8.0 0.7 all-gather.5.cloned.1.call-update
  8.7 0.5 collective-permute-start
  9.2 37.1 %collective-permute-done = bf16[2,384,2048]{2,1,0:T(8,128)(2,1)S(1)} collective-permute-done((bf16[2,384,2048]{2,1,0:T(8,128)(2,1)}, bf16[2,384,2048]{2,1,0:T(8,128)(2,1)S(1)}, u32[]{:S(2)}, u32[]{:S(2)}) %collective-permute-start) | collective-permute-done | bytes 3145760 | tf_op jit(solution)/shard_map/ppermute | solution.py:27
  46.3 0.0 collective-permute-start.1
  46.4 0.6 gather_fusion
  47.0 17.1 %all_gather.15 = bf16[4,4,512]{2,1,0:T(4,128)(2,1)S(1)} all-gather(bf16[1,4,512]{2,1,0:T(4,128)(2,1)} %param.21), channel_id=1, replica_groups=mesh['groups'=2,'cand'=4,'tensor'=4] {'cand'}, dimensions={0}, use_global_device_ids=true | all-gather | bytes 20480 | tf_op jit(solution)/shard_map/all_gather | solution.py:95
  64.1 0.8 fusion.26
  64.9 0.6 gather_fusion.2
  65.5 0.1 broadcast_select_fusion
  65.6 17.5 %collective-permute-done.1 = bf16[2,384,2048]{2,1,0:T(8,128)(2,1)} collective-permute-done((bf16[2,384,2048]{2,1,0:T(8,128)(2,1)S(1)}, bf16[2,384,2048]{2,1,0:T(8,128)(2,1)}, u32[]{:S(2)}, u32[]{:S(2)}) %collective-permute-start.1) | collective-permute-done | bytes 3145760 | tf_op jit(solution)/shard_map/ppermute | solution.py:27
  83.2 6.3 %copy.40 = bf16[2,2048,512]{1,2,0:T(8,128)(2,1)} copy(bf16[2,2048,512]{2,1,0:T(8,128)(2,1)} %param.15) | data formatting | bytes 8388608 | tf_op args[3]
  89.5 18.4 %all_gather.14 = bf16[4,4,1024]{2,1,0:T(4,128)(2,1)S(1)} all-gather(bf16[1,4,1024]{2,1,0:T(4,128)(2,1)S(1)} %copy-done.5), channel_id=1, replica_groups=mesh['groups'=2,'cand'=4,'tensor'=4] {'cand'}, dimensions={0}, use_global_device_ids=true | all-gather | bytes 40960 | tf_op jit(solution)/shard_map/all_gather | solution.py:94
  107.9 0.6 gather_fusion.1
  108.5 0.3 fusion.36
  108.9 0.1 iota_compare_fusion.1
  108.9 0.0 copy-start.7
  109.0 4.7 fusion.34
  113.7 0.8 fusion.35
  114.5 0.1 fusion.22
  114.6 0.4 fusion.18
  115.0 0.6 fusion.13
  115.6 0.3 fusion.15
  115.9 0.3 convolution_convert_fusion.2
  116.3 1.2 concatenate.14
  117.5 0.6 dynamic-slice
  118.1 25.4 %all-reduce.1 = bf16[4,4,1024]{2,1,0:T(4,128)(2,1)S(1)} all-reduce(bf16[4,4,1024]{2,1,0:T(4,128)(2,1)S(1)} %copy.52), channel_id=2, replica_groups=mesh['groups'=2,'cand'=4,'tensor'=4] {'cand'}, use_global_device_ids=true, to_apply=%region_10.11.clone | all-reduce | flops 16384 | bytes 65536
  143.5 1.2 constant_dynamic-slice_fusion.2
  144.8 2.4 constant_dynamic-update-slice_fusion.7
  147.2 2.3 constant_dynamic-update-slice_fusion.6
  149.5 0.2 constant_dynamic-update-slice_fusion.5
  149.7 0.4 constant_dynamic-update-slice_fusion.4
  150.2 2.3 constant_dynamic-update-slice_fusion.3
  152.5 2.3 constant_dynamic-update-slice_fusion.2
  154.8 0.2 constant_dynamic-update-slice_fusion.1
  155.0 0.4 constant_dynamic-update-slice_fusion
  155.4 5.3 constant_dynamic-slice_fusion.3
  160.7 2.9 all-gather.3.cloned.1.call-done
  163.6 12.0 %convolution_convert_fusion.1 = bf16[768,512]{1,0:T(8,128)(2,1)S(1)} fusion(bf16[768,8192]{1,0:T(8,128)(2,1)} %bitcast.126, bf16[8192,512]{1,0:T(8,128)(2,1)} %all-gather.3.cloned.1.call-done), kind=kOutput, calls=%fused_computation.29 | convolution fusion | flops 6442844160 | bytes 21757952 | tf_op jit(solution)/shard_map/dot_general | solution.py:42
  175.6 0.2 reshape.109
  175.8 0.6 copy.41
  176.5 5.3 pad_maximum_fusion
  181.7 268.6 %all-gather.5.cloned.1.call-done = bf16[8192,1024]{1,0:T(8,128)(2,1)} async-done(((bf16[2048,1024]{1,0:T(8,128)(2,1)}), bf16[8192,1024]{1,0:T(8,128)(2,1)}) %all-gather.5.cloned.1.call-update) | async-done | bytes 16777232 | tf_op jit(solution)/shard_map/all_gather | solution.py:39
  450.3 18.7 %convolution_convert_fusion = bf16[768,1024]{1,0:T(8,128)(2,1)S(1)} fusion(bf16[768,8192]{1,0:T(8,128)(2,1)} %bitcast.127, bf16[8192,1024]{1,0:T(8,128)(2,1)} %all-gather.5.cloned.1.call-done), kind=kOutput, calls=%fused_computation.28 | convolution fusion | flops 12885688320 | bytes 30932992 | tf_op jit(solution)/shard_map/dot_general | solution.py:37
  469.1 2.4 reshape.110
  471.5 69.6 %while.10 = (s32[]{:T(128)}, f32[2,384]{1,0:T(2,128)S(1)}, bf16[2,2432,2,256]{1,3,2,0:T(8,128)(2,1)}, pred[384,2432]{0,1:T(8,128)(4,1)}, bf16[2,384,2,4,128]{4,3...) while((s32[]{:T(128)}, f32[2,384]{1,0:T(2,128)S(1)}, bf16[2,2432,2,256]{1,3,2,0:T(8,128)(2,1)}, ...), condition=%wide.region_3.4_spmd, body=%wide.region_0.3_spmd.sunk | while | flops 3874753024 | bytes 88654456 | solution.py:81
  471.5 1.9 constant_dynamic-slice_fusion.6
  473.3 2.6 copy.94
  475.9 1.4 constant_dynamic-slice_fusion.7
  477.4 17.0 %fusion.52 = (f32[2,4,384]{2,1,0:T(4,128)S(1)}, f32[2,4,384,2432]{2,3,1,0:T(8,128)}) fusion(pred[384,2432]{0,1:T(8,128)(4,1)} %get-tuple-element.139, bf16[2432,2,256]{2,0,1:T(8,128)(2,1)} %bitcast.122, bf16[1,384,2,4,128]{4,3,2,1,0:T(4,128)(2,1)S(1)} %constant_dynamic-slice_fusion.7), kind=kOutput, calls=%fused_computation.83.clone.1 | convolution fusion | flops 1942489472 | bytes 32862208 | tf_op jit(solution)/shard_map/while/body/eval_jaxpr/sub | solution.py:71
  494.4 10.9 %fusion.53 = f32[2,128,4,384]{3,1,2,0:T(8,128)S(1)} fusion(f32[2,4,384,2432]{2,3,1,0:T(8,128)} %get-tuple-element.118, f32[2,4,384]{2,1,0:T(4,128)S(1)} %get-tuple-element.119, bf16[2432,2,256]{2,0,1:T(8,128)(2,1)S(1)} %bitcast.123), kind=kOutput, calls=%fused_computation.11.clone.1 | convolution fusion | flops 1927544832 | bytes 32714752 | tf_op jit(solution)/shard_map/while/body/eval_jaxpr/kgts,skd->tkgd/dot_general | solution.py:72
  505.3 0.9 fusion.54
  506.2 0.1 dynamic_update_slice.5
  506.3 1.9 constant_dynamic-slice_fusion.6
  508.1 2.6 copy.94
  510.8 1.4 constant_dynamic-slice_fusion.7
  512.2 17.0 %fusion.52 = (f32[2,4,384]{2,1,0:T(4,128)S(1)}, f32[2,4,384,2432]{2,3,1,0:T(8,128)}) fusion(pred[384,2432]{0,1:T(8,128)(4,1)} %get-tuple-element.139, bf16[2432,2,256]{2,0,1:T(8,128)(2,1)} %bitcast.122, bf16[1,384,2,4,128]{4,3,2,1,0:T(4,128)(2,1)S(1)} %constant_dynamic-slice_fusion.7), kind=kOutput, calls=%fused_computation.83.clone.1 | convolution fusion | flops 1942489472 | bytes 32862208 | tf_op jit(solution)/shard_map/while/body/eval_jaxpr/sub | solution.py:71
  529.2 10.9 %fusion.53 = f32[2,128,4,384]{3,1,2,0:T(8,128)S(1)} fusion(f32[2,4,384,2432]{2,3,1,0:T(8,128)} %get-tuple-element.118, f32[2,4,384]{2,1,0:T(4,128)S(1)} %get-tuple-element.119, bf16[2432,2,256]{2,0,1:T(8,128)(2,1)S(1)} %bitcast.123), kind=kOutput, calls=%fused_computation.11.clone.1 | convolution fusion | flops 1927544832 | bytes 32714752 | tf_op jit(solution)/shard_map/while/body/eval_jaxpr/kgts,skd->tkgd/dot_general | solution.py:72
  540.1 0.9 fusion.54
  541.0 0.1 dynamic_update_slice.5
  541.1 7.4 %psum.7 = f32[2,384]{1,0:T(2,128)} all-reduce(f32[2,384]{1,0:T(2,128)S(1)} %get-tuple-element.34), channel_id=1, replica_groups=mesh['groups'=2,'cand'=4,'tensor'=4] {'tensor'}, use_global_device_ids=true, to_apply=%region_4.5 | all-reduce | flops 768 | bytes 6144 | tf_op jit(solution)/shard_map/psum | solution.py:82
  (33 shorter events, 0.2 us)
Async XLA Ops:
  7.2 39.2 %copy-start = (s32[8]{0:T(128)S(1)}, s32[8]{0:T(128)}, u32[]{:S(2)}) copy-start(s32[8]{0:T(128)} %param.18) | copy-start | bytes 100
  7.2 82.3 %copy-start.5 = (bf16[1,4,1024]{2,1,0:T(4,128)(2,1)S(1)}, bf16[1,4,1024]{2,1,0:T(4,128)(2,1)}, u32[]{:S(2)}) copy-start(bf16[1,4,1024]{2,1,0:T(4,128)(2,1)} %param.20) | copy-start | bytes 24580
  7.2 156.4 %all-gather.3.cloned.1.call-start = ((), (), s32[]{:S(2)}) async-start(), calls=%async_computation | async-start | bytes 10485760 | tf_op jit(solution)/shard_map/all_gather | solution.py:44
  7.9 442.4 %all-gather.5.cloned.1.call-start = ((), (), s32[]{:S(2)}) async-start(), calls=%async_computation.1 | async-start | bytes 20971520 | tf_op jit(solution)/shard_map/all_gather | solution.py:39
  8.7 37.6 %collective-permute-start = (bf16[2,384,2048]{2,1,0:T(8,128)(2,1)}, bf16[2,384,2048]{2,1,0:T(8,128)(2,1)S(1)}, u32[]{:S(2)}, u32[]{:S(2)}) collective-permute-start(bf16[2,384,2048]{2,1,0:T(8,128)(2,1)} %param.12), channel_id=1, source_target_pairs={{0,1},{1,2},{2,3},{3,0},{4,5},{5,6},{6,7},{7,4},{8,9},{9,10},{10,1... | collective-permute-start | bytes 9437192 | tf_op jit(solution)/shard_map/ppermute | solution.py:27
  46.3 36.8 %collective-permute-start.1 = (bf16[2,384,2048]{2,1,0:T(8,128)(2,1)S(1)}, bf16[2,384,2048]{2,1,0:T(8,128)(2,1)}, u32[]{:S(2)}, u32[]{:S(2)}) collective-permute-start(bf16[2,384,2048]{2,1,0:T(8,128)(2,1)S(1)} %collective-permute-done), channel_id=1, source_target_pairs={{0,1},{1,2},{2,3},{3,0},{4,5},{5,6},{6,7},{7,4},{8,9},{9,10},{10,1... | collective-permute-start | bytes 9437192 | tf_op jit(solution)/shard_map/ppermute | solution.py:27
  83.1 61.7 %collective-permute-start.2 = (bf16[2,384,2048]{2,1,0:T(8,128)(2,1)}, bf16[2,384,2048]{2,1,0:T(8,128)(2,1)}, u32[]{:S(2)}, u32[]{:S(2)}) collective-permute-start(bf16[2,384,2048]{2,1,0:T(8,128)(2,1)} %collective-permute-done.1), channel_id=1, source_target_pairs={{0,1},{1,2},{2,3},{3,0},{4,5},{5,6},{6,7},{7,4},{8,9},{9,10},{10,1... | collective-permute-start | bytes 9437192 | tf_op jit(solution)/shard_map/ppermute | solution.py:27
  89.5 26.4 %copy-start.6 = (s32[4]{0:T(128)S(1)}, s32[4]{0:T(128)}, u32[]{:S(2)}) copy-start(s32[4]{0:T(128)} %param.19) | copy-start | bytes 52
  108.9 8.6 %copy-start.7 = (u32[32]{0:T(128)S(1)}, u32[32]{0:T(128)}, u32[]{:S(2)}) copy-start(u32[32]{0:T(128)} %constant.119) | copy-start | bytes 388
  144.7 5.0 copy-start.3
  181.7 289.7 %copy-start.4 = (f32[1024]{0:T(1024)S(1)}, f32[1024]{0:T(1024)}, u32[]{:S(2)}) copy-start(f32[1024]{0:T(1024)} %param.16) | copy-start | bytes 12292
  477.4 17.0 %copy-start.2 = (bf16[1,2432,2,256]{3,1,2,0:T(8,128)(2,1)S(1)}, bf16[1,2432,2,256]{3,1,2,0:T(8,128)(2,1)}, u32[]{:S(2)}) copy-start(bf16[1,2432,2,256]{3,1,2,0:T(8,128)(2,1)} %copy.94) | copy-start | bytes 7471108 | tf_op jit(solution)/shard_map/while
  512.2 17.0 %copy-start.2 = (bf16[1,2432,2,256]{3,1,2,0:T(8,128)(2,1)S(1)}, bf16[1,2432,2,256]{3,1,2,0:T(8,128)(2,1)}, u32[]{:S(2)}) copy-start(bf16[1,2432,2,256]{3,1,2,0:T(8,128)(2,1)} %copy.94) | copy-start | bytes 7471108 | tf_op jit(solution)/shard_map/while
  541.1 7.4 %copy-start.1 = (s32[8]{0:T(128)S(1)}, s32[8]{0:T(128)}, u32[]{:S(2)}) copy-start(s32[8]{0:T(128)} %param.18) | copy-start | bytes 100
Sparse Core Ops, SparseCore 0:
  9.6 153.9 all-gather.2
  165.2 285.1 all-gather.4
